TPU v7x, 512 devices: a whole 4x4x16 slice. The times are simulated.
512 devices in a mesh: rep: 64 (over z, y_lo, core), fsdp: 8 (over y_hi, x).
Axes of the slice: x: 4, y: 4 (y_hi: 2, y_lo: 2; y = y_hi * 2 + y_lo), z: 16, core: 2. Of those that a mesh axis runs over, the one named last changes fastest.
Arguments:
- tokens: bfloat16 [131072, 4096], P(('rep', 'fsdp')), may hold values from -6 to 6
- weights: float32 [64, 4096, 512], P('rep', 'fsdp'), may hold values from -6 to 6
- verdict_head: bfloat16 [512, 128], replicated
- verdict: int32 [131072], P(('rep', 'fsdp')), may hold values from 0 to 127
- step_index: int32 [1], replicated, may hold values from 0 to 999
Outputs:
- mixed_weights: float32 [64, 4096, 512], P('rep', 'fsdp')
- token_loss: float32 [131072], P(('rep', 'fsdp'))
All inputs are finite; a program needn't handle non-finite values.
Results may differ from a plain program's by a relative error of at most 0.012.
The roundings to bfloat16 on the way count: a program that leaves them out, or rounds other values in their place, can miss the bound.
Values may be sent and summed in bfloat16 or wider, within the bound.
A program may use at most 64 MiB of HBM per device.

v0:
```python
from functools import partial

import jax
import jax.numpy as jnp
from jax import lax
from jax.sharding import PartitionSpec as P

eps_value = 1e-06
step_size = 8.0


def for_sending(value):

    def short(part):
        return part.astype(jnp.bfloat16) if part.dtype == jnp.float32 else part

    return jax.tree.map(short, value)


def from_behind(block, axis, distance):
    devices = range(lax.axis_size(axis))
    route = [((i - distance) % len(devices), i) for i in devices]
    return lax.ppermute(block, axis, route)


def head_gradient(values, verdict, verdict_head, inv_root):
    mean_square = jnp.mean(values * values, axis=-1, keepdims=True)
    recip = lax.rsqrt(mean_square + eps_value)
    normed = values * recip
    logits = jnp.dot(normed.astype(jnp.bfloat16), verdict_head, preferred_element_type=jnp.float32)
    total = jax.nn.logsumexp(logits, axis=-1)
    labels = jnp.arange(logits.shape[1], dtype=jnp.int32)[None, :] == verdict[:, None]
    chosen = jnp.sum(jnp.where(labels, logits, jnp.zeros_like(logits)), axis=-1)
    token_loss = total - chosen
    dlogits = (jax.nn.softmax(logits, axis=-1) - labels.astype(logits.dtype)).astype(jnp.bfloat16)
    along = jnp.dot(dlogits, verdict_head.T, preferred_element_type=jnp.float32)
    projected = jnp.mean(normed * along, axis=-1, keepdims=True)
    grad_values = ((along - normed * projected) * recip * inv_root).astype(jnp.bfloat16)
    return (token_loss, grad_values)


def send_updated(block_rows, level):
    return jax.tree.map(
        lambda part, own: part.astype(own.dtype),
        from_behind(for_sending(block_rows), "rep", 1 << level),
        block_rows,
    )


def local(tokens, weights, verdict_head, verdict, step_index):
    inv_root = tokens.shape[1] ** (-0.5)
    master = weights[0]
    half_rows = master.astype(jnp.bfloat16)
    levels = lax.axis_size("rep").bit_length() - 1
    level_index = step_index[0] % levels
    columns = tokens
    values = (
        jnp.dot(
            columns,
            lax.all_gather(half_rows, "fsdp", axis=0, tiled=True),
            preferred_element_type=jnp.float32,
        )
        * inv_root
    )
    token_loss, grad_values = head_gradient(values, verdict, verdict_head, inv_root)
    columns = tokens
    grad = lax.psum_scatter(
        lax.dot_general(
            columns, grad_values, (((0,), (0,)), ((), ())), preferred_element_type=jnp.float32
        ).astype(jnp.bfloat16),
        "fsdp",
        scatter_dimension=0,
        tiled=True,
    ).astype(jnp.float32)
    grad_block = grad[None]
    updated = weights - step_size * grad_block
    received = lax.switch(
        level_index, [partial(send_updated, level=lv) for lv in range(levels)], updated
    )
    mixed_weights = 0.5 * (updated + received)
    return (mixed_weights, token_loss)


def solution(mesh):
    return jax.shard_map(
        local,
        mesh=mesh,
        in_specs=(P(("rep", "fsdp"), None), P("rep", "fsdp", None), P(), P(("rep", "fsdp")), P()),
        out_specs=(P("rep", "fsdp", None), P(("rep", "fsdp"))),
        check_vma=False,
    )
```

profile of v0, /device:TPU:32, one launch (start us, length us, event | category | flops | bytes accessed | tf_op | source)
XLA Modules:
  0.0 277.7 jit_solution(3266565168649921826)
XLA Ops:
  7.2 0.0 copy-start
  7.2 0.0 all-gather.3.cloned.1.call-start
  7.2 2.2 convert_element_type.77
  9.5 0.0 all-gather.3.cloned.1.call-update
  9.5 0.0 copy-start.3
  9.5 0.0 reduce-scatter.2.cloned.1.call-start
  9.5 93.4 %all-gather.3.cloned.1.call-done = bf16[1,4096,512]{2,1,0:T(8,128)(2,1)} async-done(((bf16[1,512,512]{2,1,0:T(8,128)(2,1)}), bf16[1,4096,512]{2,1,0:T(8,128)(2,1)}) %all-gather.3.cloned.1.call-update) | async-done | bytes 4194320 | tf_op jit(solution)/shard_map/all_gather | solution.py:60
  102.9 3.5 %multiply_reduce_fusion.1 = (f32[256]{0:T(256)S(1)}, f32[256,512]{1,0:T(8,128)S(1)}) fusion(bf16[256,4096]{1,0:T(8,128)(2,1)S(1)} %copy-done, bf16[1,4096,512]{2,1,0:T(8,128)(2,1)} %all-gather.3.cloned.1.call-done), kind=kOutput, calls=%fused_computation.8 | convolution fusion | flops 1074134784 | bytes 6816768 | tf_op jit(solution)/shard_map/dot_general | solution.py:58
  106.4 0.3 fusion.15
  106.8 0.1 exponential_reduce_fusion
  106.8 0.4 multiply_reduce_fusion
  107.2 3.4 %fusion = bf16[4096,512]{0,1:T(8,128)(2,1)} fusion(bf16[256,4096]{1,0:T(8,128)(2,1)S(1)} %copy-done, f32[256,512]{1,0:T(8,128)S(1)} %get-tuple-element.40, f32[256,512]{1,0:T(8,128)S(1)} %get-tuple-element.36, f32[256]{0:T(256)S(1)} %get-tuple-element.33, f32[256]{0:T(256)S(1)} %broadcast_multiply_fusion.1, f32[256]{0:T(256)S(1)} %get-tuple-element.34), kind=kOutput, calls=%fused_computation.1 | convolution fusion | flops 1076625408 | bytes 7343104 | tf_op jit(solution)/shard_map/dot_general | solution.py:68
  110.6 0.0 reduce-scatter.2.cloned.1.call-update
  110.6 1.3 copy.7
  112.6 0.6 add_subtract_fusion
  113.2 96.4 %reduce-scatter.2.cloned.1.call-done = bf16[512,512]{0,1:T(8,128)(2,1)} async-done(((bf16[4096,512]{0,1:T(8,128)(2,1)}), bf16[512,512]{0,1:T(8,128)(2,1)}) %reduce-scatter.2.cloned.1.call-update) | async-done | bytes 524304 | tf_op jit(solution)/shard_map/reduce_scatter | solution.py:67
  209.6 1.5 bitcast_subtract_fusion
  211.2 54.7 %conditional.4 = (f32[1,512,512]{1,2,0:T(8,128)}) conditional(s32[]{:T(128)} %clamp.3, (f32[1,512,512]{1,2,0:T(8,128)S(1)}) %tuple.60, (f32[1,512,512]{1,2,0:T(8,128)S(1)}) %tuple.60, (f32[1,512,512]{1,2,0:T(8,128)S(1)}) %tuple.60, (f32[1,512,512]{1,2,0:T(8,128)S(1)}) %tuple.60, ...), branch_computations={%region_5.6_spmd, %region_6.7_spmd, %region_7.8_spmd, %region_8.9_... | conditional | bytes 5242928
  211.2 1.0 copy.26
  212.2 7.6 %collective-permute-start.4 = (bf16[1,512,512]{2,1,0:T(8,128)(2,1)}, bf16[1,512,512]{2,1,0:T(8,128)(2,1)}, u32[]{:S(2)}, u32[]{:S(2)}) collective-permute-start(bf16[1,512,512]{2,1,0:T(8,128)(2,1)} %copy.26), channel_id=1, source_target_pairs={{384,0},{392,8},{400,16},{408,24},{416,32},{424,40},{432,48},{440,... | collective-permute-start | bytes 1572872 | tf_op jit(solution)/shard_map/cond/branch_4_fun/ppermute | solution.py:23
  219.8 43.8 %collective-permute-done.4 = bf16[1,512,512]{2,1,0:T(8,128)(2,1)} collective-permute-done((bf16[1,512,512]{2,1,0:T(8,128)(2,1)}, bf16[1,512,512]{2,1,0:T(8,128)(2,1)}, u32[]{:S(2)}, u32[]{:S(2)}) %collective-permute-start.4) | collective-permute-done | bytes 524320 | tf_op jit(solution)/shard_map/cond/branch_4_fun/ppermute | solution.py:23
  263.7 2.2 copy.20
  265.9 2.4 add_multiply_fusion
  268.3 2.5 copy.15
  (9 shorter events, 0.0 us)
Async XLA Ops:
  7.2 95.7 %copy-start = (bf16[256,4096]{1,0:T(8,128)(2,1)S(1)}, bf16[256,4096]{1,0:T(8,128)(2,1)}, u32[]{:S(2)}) copy-start(bf16[256,4096]{1,0:T(8,128)(2,1)} %param.11) | copy-start | bytes 6291460
  7.2 95.7 %all-gather.3.cloned.1.call-start = ((), (), s32[]{:S(2)}) async-start(), calls=%async_computation.2 | async-start | bytes 4718592 | tf_op jit(solution)/shard_map/all_gather | solution.py:60
  9.4 97.0 %copy-start.2 = (bf16[512,128]{1,0:T(8,128)(2,1)S(1)}, bf16[512,128]{1,0:T(8,128)(2,1)}, u32[]{:S(2)}) copy-start(bf16[512,128]{1,0:T(8,128)(2,1)} %param.13) | copy-start | bytes 393220
  9.5 97.3 %copy-start.3 = (s32[256]{0:T(256)S(1)}, s32[256]{0:T(256)}, u32[]{:S(2)}) copy-start(s32[256]{0:T(256)} %param.14) | copy-start | bytes 3076
  9.5 200.1 %reduce-scatter.2.cloned.1.call-start = ((), (), s32[]{:S(2)}) async-start(), calls=%async_computation.1 | async-start | bytes 4718592 | tf_op jit(solution)/shard_map/reduce_scatter | solution.py:67
  107.2 3.4 %copy-start.1 = (f32[1,512,512]{2,1,0:T(8,128)S(1)}, f32[1,512,512]{2,1,0:T(8,128)}, u32[]{:S(2)}) copy-start(f32[1,512,512]{2,1,0:T(8,128)} %param.12) | copy-start | bytes 3145732
  212.2 51.5 %collective-permute-start.4 = (bf16[1,512,512]{2,1,0:T(8,128)(2,1)}, bf16[1,512,512]{2,1,0:T(8,128)(2,1)}, u32[]{:S(2)}, u32[]{:S(2)}) collective-permute-start(bf16[1,512,512]{2,1,0:T(8,128)(2,1)} %copy.26), channel_id=1, source_target_pairs={{384,0},{392,8},{400,16},{408,24},{416,32},{424,40},{432,48},{440,... | collective-permute-start | bytes 1572872 | tf_op jit(solution)/shard_map/cond/branch_4_fun/ppermute | solution.py:23
Sparse Core Ops, SparseCore 0:
  11.8 91.0 all-gather.2
  110.8 98.8 reduce-scatter.1
where the time goes:
time: 278 us
  waiting for transfers between devices  234 us (84%)
  between operations  14.8 us (5%)
  starting transfers between devices  7.71 us (3%)
  matrix products  7.57 us (3%)
  local copies, waits for them, and re-layouts  7.08 us (3%)
  other arithmetic  6.83 us (2%)
    reduce_scatter x1, waiting for transfers between devices, local(): lax.psum_scatter(lax.dot_general(columns, grad_values, (((0,), (0,)), (()...  96.4 us
    all_gather x1, waiting for transfers between devices, local(): lax.all_gather(half_rows, 'fsdp', axis=0, tiled=True)  93.4 us
    ppermute x1, waiting for transfers between devices, from_behind(): return lax.ppermute(block, axis, route)  43.8 us
    ppermute x1, starting transfers between devices, from_behind(): return lax.ppermute(block, axis, route)  7.63 us
  transfers between devices with their start and end apart: 3, of which 3 were waited for; matrix products, arithmetic and copies ran while one was open for 1% of the time, Pallas kernels for 0%

commit v1 on v0

v1 whole, which is shorter than its diff:
```python
import functools

import jax
import jax.numpy as jnp
from jax import lax
from jax.experimental import pallas as pl
from jax.experimental.pallas import tpu as pltpu
from jax.sharding import PartitionSpec as P

MESH = pl.DeviceIdType.MESH
EPS = 1e-06
STEP = 8.0
NX = 4
CHUNKS = 4


def tdot(a, b):
    return lax.dot_general(a, b, (((0,), (0,)), ((), ())), preferred_element_type=jnp.float32)


def kernel(inv_root, tok_hbm, w_hbm, head_ref, verdict_ref, upd_ref, half_ref, loss_ref,
           tok, tok_y, wv, wall, acc, labels, psend, precv, gsend, grecv, own, opp, sides,
           opp_in, side_in, local_sem, tok_ss, tok_rs, w_ss, w_rs, p_ss, p_rs, g_ss, g_rs,
           o_ss, o_rs, s_ss, s_rs):
    rep, me = lax.axis_index("rep"), lax.axis_index("fsdp")
    row, x = me // NX, me % NX
    pair = (1 - row) * NX + x
    xs = [row * NX + (x + 1) % NX, row * NX + (x + NX - 1) % NX]
    depth, kv = wv.shape
    half = depth // 2
    rows = tok.shape[0]
    wide = NX * depth
    part = rows // CHUNKS

    def remote(src, dst, ss, rs, peer):
        return pltpu.make_async_remote_copy(src_ref=src, dst_ref=dst, send_sem=ss, recv_sem=rs,
                                            device_id=(rep, peer), device_id_type=MESH)

    def block(of):
        return pl.multiple_of(((x + of + NX) % NX) * depth, depth)

    w_in = pltpu.make_async_copy(w_hbm, wv, local_sem.at[0])
    w_in.start()
    t_in = pltpu.make_async_copy(tok_hbm.at[:, pl.ds(pl.multiple_of(row * wide, wide), wide)], tok,
                                 local_sem.at[1])
    t_in.start()
    barrier = pltpu.get_barrier_semaphore()
    for peer in xs + [pair]:
        pl.semaphore_signal(barrier, inc=1, device_id=(rep, peer), device_id_type=MESH)
    w_in.wait()
    wall[pl.ds(block(0), depth), :] = wv[...].astype(jnp.bfloat16)
    pl.semaphore_wait(barrier, 3)

    tok_out = []
    for c in range(CHUNKS):
        copy = remote(
            tok_hbm.at[pl.ds(c * part, part), pl.ds(pl.multiple_of((1 - row) * wide, wide), wide)],
            tok_y.at[pl.ds(c * part, part), :], tok_ss.at[c], tok_rs.at[c], pair)
        tok_out.append(copy)

    def w_copy(d, stage):
        hop = d if stage in (0, 2) else 1 - d
        of = 0 if stage < 2 else (-1 if d == 0 else 1)
        where = pl.ds(pl.multiple_of(block(of) + hop * half, half), half)
        return remote(wall.at[where, :], wall.at[where, :], w_ss.at[d, stage], w_rs.at[d, stage], xs[d])

    w_out = [[w_copy(d, s) for s in range(3)] for d in range(2)]
    for d in range(2):
        w_out[d][0].start()
    for copy in tok_out:
        copy.start()
    for d in range(2):
        w_out[d][1].start()

    hit = lax.broadcasted_iota(jnp.int32, (labels.shape[1], rows), 0) == verdict_ref[...]
    labels[...] = jnp.transpose(hit.astype(jnp.float32))
    t_in.wait()

    def product(of):
        return jnp.dot(tok[:, pl.ds(block(of), depth)], wall[pl.ds(block(of), depth), :],
                       preferred_element_type=jnp.float32)

    acc[...] = product(0)
    for d in range(2):
        w_out[d][0].wait_recv()
        w_out[d][2].start()
    for d in range(2):
        w_out[d][1].wait_recv()
    acc[...] += product(-1) + product(1)
    for d in range(2):
        w_out[d][2].wait_recv()
    acc[...] += product(2)

    p_out = []
    for c in range(CHUNKS):
        here = pl.ds(c * part, part)
        tok_out[c].wait_recv()
        psend[here, :] = jnp.dot(tok_y[here, :], wall[...],
                                 preferred_element_type=jnp.float32).astype(jnp.bfloat16)
        copy = remote(psend.at[here, :], precv.at[here, :], p_ss.at[c], p_rs.at[c], pair)
        copy.start()
        p_out.append(copy)
    for copy in p_out:
        copy.wait_recv()

    values = (acc[...] + precv[...].astype(jnp.float32)) * inv_root
    recip = lax.rsqrt(jnp.mean(values * values, axis=-1, keepdims=True) + EPS)
    normed = values * recip
    logits = jnp.dot(normed.astype(jnp.bfloat16), head_ref[...], preferred_element_type=jnp.float32)
    top = jnp.max(logits, axis=-1, keepdims=True)
    powers = jnp.exp(logits - top)
    total = jnp.sum(powers, axis=-1, keepdims=True)
    chosen = jnp.sum(logits * labels[...], axis=-1, keepdims=True)
    dlogits = (powers / total - labels[...]).astype(jnp.bfloat16)
    along = lax.dot_general(dlogits, head_ref[...], (((1,), (1,)), ((), ())),
                            preferred_element_type=jnp.float32)
    projected = jnp.mean(normed * along, axis=-1, keepdims=True)
    gsend[...] = ((along - normed * projected) * recip * inv_root).astype(jnp.bfloat16)
    g_out = remote(gsend, grecv, g_ss.at[0], g_rs.at[0], pair)
    g_out.start()
    loss = jnp.log(total) + top - chosen
    loss_ref[...] = jnp.transpose(jnp.broadcast_to(loss, (rows, 128)))[0:1, :]

    for k, of in enumerate((2, 1, -1, 0)):
        own[k] = tdot(tok[:, pl.ds(block(of), depth)], gsend[...]).astype(jnp.bfloat16)
    g_out.wait_recv()

    def summed(k, of):
        other = tdot(tok_y[:, pl.ds(block(of), depth)], grecv[...]).astype(jnp.bfloat16)
        return own[k].astype(jnp.float32) + other.astype(jnp.float32)

    opp[...] = summed(0, 2).astype(jnp.bfloat16)
    o_out = []
    for d in range(2):
        copy = remote(opp.at[pl.ds(d * half, half), :], opp_in.at[d], o_ss.at[d], o_rs.at[d], xs[d])
        copy.start()
        o_out.append(copy)
    s_out = [[None, None], [None, None]]
    for d in range(2):
        sides[d] = summed(1 + d, 1 - 2 * d).astype(jnp.bfloat16)
        for h in range(2):
            at = pl.ds(h * half, half)
            s_out[d][h] = remote(sides.at[d, at, :], side_in.at[d, at, :], s_ss.at[d, h], s_rs.at[d, h], xs[d])
        s_out[d][1 - d].start()
    for d in range(2):
        at = pl.ds(d * half, half)
        o_out[d].wait_recv()
        sides[d, at, :] = (sides[d, at, :].astype(jnp.float32)
                           + opp_in[d].astype(jnp.float32)).astype(jnp.bfloat16)
        s_out[d][d].start()
    acc2 = upd_ref
    acc2[...] = summed(3, 0)
    for d in range(2):
        for h in range(2):
            s_out[d][h].wait_recv()
    grad = acc2[...] + side_in[0].astype(jnp.float32) + side_in[1].astype(jnp.float32)
    updated = wv[...] - STEP * grad
    upd_ref[...] = updated
    half_ref[...] = updated.astype(jnp.bfloat16)
    for copy in tok_out + w_out[0] + w_out[1] + p_out + [g_out] + o_out + s_out[0] + s_out[1]:
        copy.wait_send()


def step_call(tokens, weights, head, verdict):
    rows, wide = tokens.shape
    depth, kv = weights.shape
    grades = head.shape[1]
    any_spec = pl.BlockSpec(memory_space=pl.ANY)
    vmem = pl.BlockSpec(memory_space=pltpu.VMEM)
    bf16, f32 = jnp.bfloat16, jnp.float32
    sem = pltpu.SemaphoreType.DMA
    return pl.pallas_call(
        functools.partial(kernel, wide ** (-0.5)),
        out_shape=(jax.ShapeDtypeStruct((depth, kv), f32), jax.ShapeDtypeStruct((depth, kv), bf16),
                   jax.ShapeDtypeStruct((1, rows), f32)),
        in_specs=[any_spec, any_spec, vmem, vmem],
        out_specs=(vmem, vmem, vmem),
        scratch_shapes=[
            pltpu.VMEM((rows, NX * depth), bf16), pltpu.VMEM((rows, NX * depth), bf16),
            pltpu.VMEM((depth, kv), f32), pltpu.VMEM((NX * depth, kv), bf16),
            pltpu.VMEM((rows, kv), f32), pltpu.VMEM((rows, grades), f32),
            pltpu.VMEM((rows, kv), bf16), pltpu.VMEM((rows, kv), bf16),
            pltpu.VMEM((rows, kv), bf16), pltpu.VMEM((rows, kv), bf16),
            pltpu.VMEM((NX, depth, kv), bf16), pltpu.VMEM((depth, kv), bf16),
            pltpu.VMEM((2, depth, kv), bf16), pltpu.VMEM((2, depth // 2, kv), bf16),
            pltpu.VMEM((2, depth, kv), bf16),
            sem((2,)), sem((CHUNKS,)), sem((CHUNKS,)), sem((2, 3)), sem((2, 3)),
            sem((CHUNKS,)), sem((CHUNKS,)), sem((1,)), sem((1,)), sem((2,)), sem((2,)),
            sem((2, 2)), sem((2, 2)),
        ],
        compiler_params=pltpu.CompilerParams(collective_id=0, has_side_effects=True,
                                             vmem_limit_bytes=48 << 20),
        name="step",
    )(tokens, weights, head, verdict)


def from_behind(value, distance):
    n = lax.axis_size("rep")
    return lax.ppermute(value, "rep", [((i - distance) % n, i) for i in range(n)])


def local(tokens, weights, verdict_head, verdict, step_index):
    levels = lax.axis_size("rep").bit_length() - 1
    level = step_index[0] % levels
    updated, sent, loss = step_call(tokens, weights[0], verdict_head, verdict[None, :])
    received = lax.switch(level, [functools.partial(from_behind, distance=1 << lv) for lv in range(levels)], sent)
    mixed = 0.5 * (updated + received.astype(jnp.float32))
    return mixed[None], loss.reshape(-1)


def solution(mesh):
    return jax.shard_map(
        local,
        mesh=mesh,
        in_specs=(P(("rep", "fsdp"), None), P("rep", "fsdp", None), P(), P(("rep", "fsdp")), P()),
        out_specs=(P("rep", "fsdp", None), P(("rep", "fsdp"))),
        check_vma=False,
    )
```

time: 278 us -> 130 us (0.47)
  waiting for transfers between devices: 234 us -> 44.1 us
  Pallas kernels: 0 us -> 62.2 us
  between operations: 14.8 us -> 1.32 us
  matrix products: 7.57 us -> 0 us
  starting transfers between devices: 7.71 us -> 14.8 us
  other arithmetic: 6.83 us -> 2.18 us
    reduce_scatter x1 -> x0, waiting for transfers between devices: 96.4 us -> none  [local(): lax.psum_scatter(lax.dot_general(columns, grad_values, (((0,), (0,)), (()...]
    all_gather x1 -> x0, waiting for transfers between devices: 93.4 us -> none  [local(): lax.all_gather(half_rows, 'fsdp', axis=0, tiled=True)]
    pallas_call x0 -> x1, Pallas kernels: none -> 62.2 us  [step_call(): pl.pallas_call(functools.partial(kernel, wide ** (-0.5)), out_shape=(jax....]
    dot_general x4 -> x0, matrix products: 7.57 us -> none  [the longest x1 3.51 us: local(): jnp.dot(columns, lax.all_gather(half_rows, 'fsdp', axis=0, tiled=True), p...]
    ppermute x1, starting transfers between devices: 7.63 us -> 14.8 us  [from_behind(): lax.ppermute(value, 'rep', [((i - distance) % n, i) for i in range(n)])]
  transfers between devices with their start and end apart: 3 -> 1, of which waited for: 3 -> 1; matrix products, arithmetic and copies ran while one was open for 1% -> 0% of each run, Pallas kernels for 0% -> 0%
where the time goes in v1:
time: 130 us
  Pallas kernels  62.2 us (48%)
  waiting for transfers between devices  44.1 us (34%)
  starting transfers between devices  14.8 us (11%)
  local copies, waits for them, and re-layouts  4.95 us (4%)
  other arithmetic  2.18 us (2%)
  between operations  1.32 us (1%)
    pallas_call x1, Pallas kernels, step_call(): pl.pallas_call(functools.partial(kernel, wide ** (-0.5)), out_shape=(jax....  62.2 us
    ppermute x1, waiting for transfers between devices, from_behind(): lax.ppermute(value, 'rep', [((i - distance) % n, i) for i in range(n)])  44.1 us
    ppermute x1, starting transfers between devices, from_behind(): lax.ppermute(value, 'rep', [((i - distance) % n, i) for i in range(n)])  14.8 us
    unnamed x9, local copies, waits for them, and re-layouts  4.95 us
  transfers between devices with their start and end apart: 1, of which 1 were waited for; matrix products, arithmetic and copies ran while one was open for 0% of the time, Pallas kernels for 0%

profile of v1, /device:TPU:32, one launch (start us, length us, event | category | flops | bytes accessed | tf_op | source)
XLA Modules:
  0.0 129.6 jit_solution(16846421061760698280)
XLA Ops:
  1.3 0.0 copy-start
  1.3 1.6 %copy-done = bf16[256,4096]{1,0:T(8,128)(2,1)S(1)} copy-done((bf16[256,4096]{1,0:T(8,128)(2,1)S(1)}, bf16[256,4096]{1,0:T(8,128)(2,1)}, u32[]{:S(2)}) %copy-start) | copy-done | bytes 2097176
  2.9 0.0 copy-start.1
  2.9 1.2 copy-done.1
  4.1 0.0 copy-start.2
  4.1 0.9 copy-done.2
  5.0 0.0 copy-start.3
  5.0 0.7 copy-done.3
  5.7 62.2 %step.1 = (f32[512,512]{1,0:T(8,128)S(1)}, bf16[512,512]{1,0:T(8,128)(2,1)S(1)}, f32[1,256]{1,0:T(1,128)S(1)}) custom-call(bf16[256,4096]{1,0:T(8,128)(2,1)S(1)} %copy-done, f32[512,512]{1,0:T(8,128)S(1)} %bitcast.6, bf16[512,128]{1,0:T(8,128)(2,1)S(1)} %copy-done.2, s32[1,256]{1,0:T(1,128)S(1)} %bitcast.7), custom_call_target="tpu_custom_call" | custom-call | tf_op jit(solution)/shard_map/step/pallas_call | solution.py:172
  67.9 59.0 %conditional.4 = (bf16[512,512]{1,0:T(8,128)(2,1)}) conditional(s32[]{:T(128)} %clamp.3, bf16[512,512]{1,0:T(8,128)(2,1)S(1)} %get-tuple-element.25, bf16[512,512]{1,0:T(8,128)(2,1)S(1)} %get-tuple-element.25, bf16[512,512]{1,0:T(8,128)(2,1)S(1)} %get-tuple-element.25, ...), branch_computations={%region_0.1_spmd, %region_1.2_spmd, %region_2.3_spmd, %region_3.4_... | conditional | bytes 2097200
  67.9 14.8 %collective-permute-start.5 = (bf16[512,512]{1,0:T(8,128)(2,1)S(1)}, bf16[512,512]{1,0:T(8,128)(2,1)}, u32[]{:S(2)}, u32[]{:S(2)}) collective-permute-start(bf16[512,512]{1,0:T(8,128)(2,1)S(1)} %param.5), channel_id=1, source_target_pairs={{256,0},{264,8},{272,16},{280,24},{288,32},{296,40},{304,48},{312,... | collective-permute-start | bytes 1572872 | tf_op jit(solution)/shard_map/cond/branch_5_fun/ppermute | solution.py:199
  82.8 44.1 %collective-permute-done.5 = bf16[512,512]{1,0:T(8,128)(2,1)} collective-permute-done((bf16[512,512]{1,0:T(8,128)(2,1)S(1)}, bf16[512,512]{1,0:T(8,128)(2,1)}, u32[]{:S(2)}, u32[]{:S(2)}) %collective-permute-start.5) | collective-permute-done | bytes 524320 | tf_op jit(solution)/shard_map/cond/branch_5_fun/ppermute | solution.py:199
  126.8 2.2 %multiply_bitcast_fusion = f32[1,512,512]{2,1,0:T(8,128)} fusion(f32[512,512]{1,0:T(8,128)S(1)} %get-tuple-element.24, bf16[512,512]{1,0:T(8,128)(2,1)} %get-tuple-element.31), kind=kLoop, calls=%fused_computation | loop fusion | flops 786432 | bytes 2621440 | tf_op jit(solution)/shard_map/broadcast_in_dim | solution.py:208
  129.0 0.6 copy.15
Async XLA Ops:
  1.3 1.6 %copy-start = (bf16[256,4096]{1,0:T(8,128)(2,1)S(1)}, bf16[256,4096]{1,0:T(8,128)(2,1)}, u32[]{:S(2)}) copy-start(bf16[256,4096]{1,0:T(8,128)(2,1)} %tok_hbm.1) | copy-start | bytes 6291460
  2.9 1.2 copy-start.1
  4.1 0.9 copy-start.2
  5.0 0.7 copy-start.3
  67.9 58.9 %collective-permute-start.5 = (bf16[512,512]{1,0:T(8,128)(2,1)S(1)}, bf16[512,512]{1,0:T(8,128)(2,1)}, u32[]{:S(2)}, u32[]{:S(2)}) collective-permute-start(bf16[512,512]{1,0:T(8,128)(2,1)S(1)} %param.5), channel_id=1, source_target_pairs={{256,0},{264,8},{272,16},{280,24},{288,32},{296,40},{304,48},{312,... | collective-permute-start | bytes 1572872 | tf_op jit(solution)/shard_map/cond/branch_5_fun/ppermute | solution.py:199

commit v2 on v1

v2 whole, which is shorter than its diff:
```python
import functools

import jax
import jax.numpy as jnp
from jax import lax
from jax.experimental import pallas as pl
from jax.experimental.pallas import tpu as pltpu
from jax.sharding import PartitionSpec as P

MESH = pl.DeviceIdType.MESH
EPS = 1e-06
STEP = 8.0
NX = 4
CHUNKS = 4
SLABS = 2
VMEM_BYTES = 64000 << 10


def tdot(a, b):
    return lax.dot_general(a, b, (((0,), (0,)), ((), ())), preferred_element_type=jnp.float32)


def kernel(inv_root, distance, tok_hbm, w_hbm, head_ref, verdict_ref, mixed_ref, loss_ref,
           tok, tok_y, wv, wall, acc, labels, psend, precv, gsend, grecv, own, mine, opp, sides,
           opp_in, side_in, mix_out, mix_in, local_sem, tok_ss, tok_rs, w_ss, w_rs, p_ss, p_rs,
           g_ss, g_rs, o_ss, o_rs, s_ss, s_rs, m_ss, m_rs):
    rep, me = lax.axis_index("rep"), lax.axis_index("fsdp")
    row, x = me // NX, me % NX
    pair = (1 - row) * NX + x
    xs = [row * NX + (x + 1) % NX, row * NX + (x + NX - 1) % NX]
    depth, kv = wv.shape
    half = depth // 2
    rows = tok.shape[0]
    wide = NX * depth
    part = rows // CHUNKS

    n_rep = lax.axis_size("rep")
    ahead, behind = (rep + distance) % n_rep, (rep + n_rep - distance) % n_rep
    cols = kv // SLABS

    def remote(src, dst, ss, rs, peer, of_rep=None):
        return pltpu.make_async_remote_copy(src_ref=src, dst_ref=dst, send_sem=ss, recv_sem=rs,
                                            device_id=(rep if of_rep is None else of_rep, peer),
                                            device_id_type=MESH)

    def block(of):
        return pl.multiple_of(((x + of + NX) % NX) * depth, depth)

    w_in = pltpu.make_async_copy(w_hbm, wv, local_sem.at[0])
    w_in.start()
    t_in = pltpu.make_async_copy(tok_hbm.at[:, pl.ds(pl.multiple_of(row * wide, wide), wide)], tok,
                                 local_sem.at[1])
    t_in.start()
    barrier = pltpu.get_barrier_semaphore()
    for peer in xs + [pair]:
        pl.semaphore_signal(barrier, inc=1, device_id=(rep, peer), device_id_type=MESH)
    pl.semaphore_signal(barrier, inc=1, device_id=(behind, me), device_id_type=MESH)
    w_in.wait()
    wall[pl.ds(block(0), depth), :] = wv[...].astype(jnp.bfloat16)
    pl.semaphore_wait(barrier, 4)

    tok_out = []
    for c in range(CHUNKS):
        copy = remote(
            tok_hbm.at[pl.ds(c * part, part), pl.ds(pl.multiple_of((1 - row) * wide, wide), wide)],
            tok_y.at[pl.ds(c * part, part), :], tok_ss.at[c], tok_rs.at[c], pair)
        tok_out.append(copy)

    def w_copy(d, stage):
        hop = d if stage in (0, 2) else 1 - d
        of = 0 if stage < 2 else (-1 if d == 0 else 1)
        where = pl.ds(pl.multiple_of(block(of) + hop * half, half), half)
        return remote(wall.at[where, :], wall.at[where, :], w_ss.at[d, stage], w_rs.at[d, stage], xs[d])

    w_out = [[w_copy(d, s) for s in range(3)] for d in range(2)]
    for d in range(2):
        w_out[d][0].start()
    for copy in tok_out:
        copy.start()
    for d in range(2):
        w_out[d][1].start()

    hit = lax.broadcasted_iota(jnp.int32, (labels.shape[1], rows), 0) == verdict_ref[...]
    labels[...] = jnp.transpose(hit.astype(jnp.float32))
    t_in.wait()

    def product(of):
        return jnp.dot(tok[:, pl.ds(block(of), depth)], wall[pl.ds(block(of), depth), :],
                       preferred_element_type=jnp.float32)

    acc[...] = product(0)
    for d in range(2):
        w_out[d][0].wait_recv()
        w_out[d][2].start()
    for d in range(2):
        w_out[d][1].wait_recv()
    acc[...] += product(-1) + product(1)
    for d in range(2):
        w_out[d][2].wait_recv()
    acc[...] += product(2)

    p_out = []
    for c in range(CHUNKS):
        here = pl.ds(c * part, part)
        tok_out[c].wait_recv()
        psend[here, :] = jnp.dot(tok_y[here, :], wall[...],
                                 preferred_element_type=jnp.float32).astype(jnp.bfloat16)
        copy = remote(psend.at[here, :], precv.at[here, :], p_ss.at[c], p_rs.at[c], pair)
        copy.start()
        p_out.append(copy)
    for copy in p_out:
        copy.wait_recv()

    values = (acc[...] + precv[...].astype(jnp.float32)) * inv_root
    recip = lax.rsqrt(jnp.mean(values * values, axis=-1, keepdims=True) + EPS)
    normed = values * recip
    logits = jnp.dot(normed.astype(jnp.bfloat16), head_ref[...], preferred_element_type=jnp.float32)
    top = jnp.max(logits, axis=-1, keepdims=True)
    powers = jnp.exp(logits - top)
    total = jnp.sum(powers, axis=-1, keepdims=True)
    chosen = jnp.sum(logits * labels[...], axis=-1, keepdims=True)
    dlogits = (powers / total - labels[...]).astype(jnp.bfloat16)
    along = lax.dot_general(dlogits, head_ref[...], (((1,), (1,)), ((), ())),
                            preferred_element_type=jnp.float32)
    projected = jnp.mean(normed * along, axis=-1, keepdims=True)
    grad_values = ((along - normed * projected) * recip * inv_root).astype(jnp.bfloat16)
    g_out = []
    for q in range(SLABS):
        gsend[q] = grad_values[:, q * cols:(q + 1) * cols]
        copy = remote(gsend.at[q], grecv.at[q], g_ss.at[q], g_rs.at[q], pair)
        copy.start()
        g_out.append(copy)
    loss = jnp.log(total) + top - chosen
    loss_ref[...] = jnp.transpose(jnp.broadcast_to(loss, (rows, 128)))[0:1, :]

    for q in range(SLABS):
        for k, of in enumerate((2, 1, -1, 0)):
            own[q, k] = tdot(tok[:, pl.ds(block(of), depth)], gsend[q]).astype(jnp.bfloat16)

    def summed(q, k, of):
        other = tdot(tok_y[:, pl.ds(block(of), depth)], grecv[q]).astype(jnp.bfloat16)
        return own[q, k].astype(jnp.float32) + other.astype(jnp.float32)

    def half_at(h):
        return pl.ds(h * half, half)

    def opp_copy(q, d):
        return remote(opp.at[q, half_at(d), :], opp_in.at[q, d], o_ss.at[q, d], o_rs.at[q, d], xs[d])

    def side_copy(q, d, h):
        return remote(sides.at[q, d, half_at(h), :], side_in.at[q, d, half_at(h), :],
                      s_ss.at[q, d, h], s_rs.at[q, d, h], xs[d])

    def send_opposite(q):
        g_out[q].wait_recv()
        opp[q] = summed(q, 0, 2).astype(jnp.bfloat16)
        for d in range(2):
            opp_copy(q, d).start()

    def send_plain(q):
        for d in range(2):
            sides[q, d] = summed(q, 1 + d, 1 - 2 * d).astype(jnp.bfloat16)
            side_copy(q, d, 1 - d).start()

    def send_added(q):
        for d in range(2):
            opp_copy(q, d).wait_recv()
            sides[q, d, half_at(d), :] = (sides[q, d, half_at(d), :].astype(jnp.float32)
                                          + opp_in[q, d].astype(jnp.float32)).astype(jnp.bfloat16)
            side_copy(q, d, d).start()

    def mix_copy(q):
        return remote(mix_out.at[q], mix_in.at[q], m_ss.at[q], m_rs.at[q], me, ahead)

    def send_updated(q):
        for d in range(2):
            for h in range(2):
                side_copy(q, d, h).wait_recv()
        grad = mine[q] + side_in[q, 0].astype(jnp.float32) + side_in[q, 1].astype(jnp.float32)
        updated = wv[:, q * cols:(q + 1) * cols] - STEP * grad
        mix_out[q] = updated.astype(jnp.bfloat16)
        mix_copy(q).start()
        mine[q] = updated

    for q in range(SLABS):
        send_opposite(q)
        if q:
            send_added(q - 1)
        send_plain(q)
        mine[q] = summed(q, 3, 0)
    send_added(SLABS - 1)
    for q in range(SLABS):
        send_updated(q)
    for q in range(SLABS):
        mix_copy(q).wait_recv()
        mixed_ref[:, q * cols:(q + 1) * cols] = 0.5 * (mine[q] + mix_in[q].astype(jnp.float32))
    for copy in tok_out + w_out[0] + w_out[1] + p_out + g_out:
        copy.wait_send()
    for q in range(SLABS):
        for d in range(2):
            opp_copy(q, d).wait_send()
            for h in range(2):
                side_copy(q, d, h).wait_send()
        mix_copy(q).wait_send()


def step_call(level, tokens, weights, head, verdict):
    rows, wide = tokens.shape
    depth, kv = weights.shape
    grades = head.shape[1]
    cols = kv // SLABS
    any_spec = pl.BlockSpec(memory_space=pl.ANY)
    vmem = pl.BlockSpec(memory_space=pltpu.VMEM)
    bf16, f32 = jnp.bfloat16, jnp.float32
    sem = pltpu.SemaphoreType.DMA
    return pl.pallas_call(
        functools.partial(kernel, wide ** (-0.5), 1 << level),
        out_shape=(jax.ShapeDtypeStruct((depth, kv), f32), jax.ShapeDtypeStruct((1, rows), f32)),
        in_specs=[any_spec, any_spec, vmem, vmem],
        out_specs=(vmem, vmem),
        scratch_shapes=[
            pltpu.VMEM((rows, NX * depth), bf16), pltpu.VMEM((rows, NX * depth), bf16),
            pltpu.VMEM((depth, kv), f32), pltpu.VMEM((NX * depth, kv), bf16),
            pltpu.VMEM((rows, kv), f32), pltpu.VMEM((rows, grades), f32),
            pltpu.VMEM((rows, kv), bf16), pltpu.VMEM((rows, kv), bf16),
            pltpu.VMEM((SLABS, rows, cols), bf16), pltpu.VMEM((SLABS, rows, cols), bf16),
            pltpu.VMEM((SLABS, NX, depth, cols), bf16), pltpu.VMEM((SLABS, depth, cols), f32),
            pltpu.VMEM((SLABS, depth, cols), bf16), pltpu.VMEM((SLABS, 2, depth, cols), bf16),
            pltpu.VMEM((SLABS, 2, depth // 2, cols), bf16), pltpu.VMEM((SLABS, 2, depth, cols), bf16),
            pltpu.VMEM((SLABS, depth, cols), bf16), pltpu.VMEM((SLABS, depth, cols), bf16),
            sem((2,)), sem((CHUNKS,)), sem((CHUNKS,)), sem((2, 3)), sem((2, 3)),
            sem((CHUNKS,)), sem((CHUNKS,)), sem((SLABS,)), sem((SLABS,)),
            sem((SLABS, 2)), sem((SLABS, 2)), sem((SLABS, 2, 2)), sem((SLABS, 2, 2)),
            sem((SLABS,)), sem((SLABS,)),
        ],
        compiler_params=pltpu.CompilerParams(collective_id=level, has_side_effects=True,
                                             vmem_limit_bytes=VMEM_BYTES),
        name="step",
    )(tokens, weights, head, verdict)


def local(tokens, weights, verdict_head, verdict, step_index):
    levels = lax.axis_size("rep").bit_length() - 1
    level = step_index[0] % levels
    mixed, loss = lax.switch(
        level, [functools.partial(step_call, lv) for lv in range(levels)],
        tokens, weights[0], verdict_head, verdict[None, :])
    return mixed[None], loss.reshape(-1)


def solution(mesh):
    return jax.shard_map(
        local,
        mesh=mesh,
        in_specs=(P(("rep", "fsdp"), None), P("rep", "fsdp", None), P(), P(("rep", "fsdp")), P()),
        out_specs=(P("rep", "fsdp", None), P(("rep", "fsdp"))),
        check_vma=False,
    )
```

time: 130 us -> 78.9 us (0.61)
  the two profiles are of different devices: /device:TPU:32 before, /device:TPU:16 now
where the time goes in v2:
time: 78.9 us; the launch traced here: 78.7 us
  Pallas kernels  75.1 us (95%)
  local copies, waits for them, and re-layouts  1.54 us (2%)
  between operations  1.3 us (2%)
    pallas_call x1, Pallas kernels, step_call(): pl.pallas_call(functools.partial(kernel, wide ** (-0.5), 1 << level), out...  75.1 us

profile of v2, /device:TPU:16, one launch (start us, length us, event | category | flops | bytes accessed | tf_op | source)
XLA Modules:
  0.0 78.7 jit_solution(4258179603688077953)
XLA Ops:
  1.3 75.8 %conditional.1 = ((f32[512,512]{1,0:T(8,128)S(1)}, f32[1,256]{1,0:T(1,128)S(1)})) conditional(s32[]{:T(128)} %clamp.3, (bf16[256,4096]{1,0:T(8,128)(2,1)}, f32[512,512]{1,0:T(8,128)}, bf16[512,128]{1,0:T(8,128)(2,1)}, s32[1,256]{1,0:T(1,128)}) %tuple.71, (bf16[256,4096]{1,0:T(8,128)(2,1)}, f32[512,512]{1,0:T(8,128)}, ...), branch_computations={%region_0.1_spmd, %region_1.2_spmd, %region_2.3_spmd, %region_3.4_... | conditional | bytes 8 | solution.py:245
  1.3 75.1 %step.7 = (f32[512,512]{1,0:T(8,128)S(1)}, f32[1,256]{1,0:T(1,128)S(1)}) custom-call(bf16[256,4096]{1,0:T(8,128)(2,1)} %get-tuple-element.68.tok_hbm, f32[512,512]{1,0:T(8,128)} %get-tuple-element.69.w_hbm, bf16[512,128]{1,0:T(8,128)(2,1)} %get-tuple-element.70.head_ref, s32[1,256]{1,0:T(1,128)} %get-tuple-element.71.verdict_ref), custom_call_target="tpu_custom_call" | custom-call | tf_op jit(solution)/shard_map/cond/branch_1_fun/step/pallas_call | solution.py:216
  77.1 1.0 %copy.22 = f32[1,512,512]{2,1,0:T(8,128)} copy(f32[1,512,512]{2,1,0:T(8,128)S(1)} %bitcast.11) | data formatting | bytes 2097152
  78.1 0.6 copy.23

commit v3 on v2

--- a/solution.py
+++ b/solution.py
@@ -22,12 +22,13 @@
 
 def kernel(inv_root, distance, tok_hbm, w_hbm, head_ref, verdict_ref, mixed_ref, loss_ref,
            tok, tok_y, wv, wall, acc, labels, psend, precv, gsend, grecv, own, mine, opp, sides,
-           opp_in, side_in, mix_out, mix_in, local_sem, tok_ss, tok_rs, w_ss, w_rs, p_ss, p_rs,
-           g_ss, g_rs, o_ss, o_rs, s_ss, s_rs, m_ss, m_rs):
+           opp_in, side_in, mix_out, mix_in, tok_x, grad_x, terms, term_out, term_in, local_sem, tok_ss, tok_rs, w_ss, w_rs, p_ss, p_rs,
+           g_ss, g_rs, o_ss, o_rs, s_ss, s_rs, m_ss, m_rs, tx_ss, tx_rs, gx_ss, gx_rs, r_ss, r_rs):
     rep, me = lax.axis_index("rep"), lax.axis_index("fsdp")
     row, x = me // NX, me % NX
     pair = (1 - row) * NX + x
     xs = [row * NX + (x + 1) % NX, row * NX + (x + NX - 1) % NX]
+    turns = {j: row * NX + (x + j) % NX for j in (1, 3, 2)}
     depth, kv = wv.shape
     half = depth // 2
     rows = tok.shape[0]
@@ -51,13 +52,18 @@
     t_in = pltpu.make_async_copy(tok_hbm.at[:, pl.ds(pl.multiple_of(row * wide, wide), wide)], tok,
                                  local_sem.at[1])
     t_in.start()
+    x_in = []
+    for k in range(2):
+        at = pl.multiple_of(((row + k) % 2 * NX + x) * depth, depth)
+        x_in.append(pltpu.make_async_copy(tok_hbm.at[:, pl.ds(at, depth)], tok_x.at[0, k], local_sem.at[2 + k]))
+        x_in[k].start()
     barrier = pltpu.get_barrier_semaphore()
-    for peer in xs + [pair]:
+    for peer in list(turns.values()) + [pair]:
         pl.semaphore_signal(barrier, inc=1, device_id=(rep, peer), device_id_type=MESH)
     pl.semaphore_signal(barrier, inc=1, device_id=(behind, me), device_id_type=MESH)
     w_in.wait()
     wall[pl.ds(block(0), depth), :] = wv[...].astype(jnp.bfloat16)
-    pl.semaphore_wait(barrier, 4)
+    pl.semaphore_wait(barrier, 5)
 
     tok_out = []
     for c in range(CHUNKS):
@@ -92,6 +98,13 @@
     for d in range(2):
         w_out[d][0].wait_recv()
         w_out[d][2].start()
+    x_out = []
+    for j, peer in turns.items():
+        for k in range(2):
+            at = pl.multiple_of(((row + k) % 2 * NX + (x + j) % NX) * depth, depth)
+            copy = remote(tok_hbm.at[:, pl.ds(at, depth)], tok_x.at[j, k], tx_ss.at[j, k], tx_rs.at[j, k], peer)
+            copy.start()
+            x_out.append(copy)
     for d in range(2):
         w_out[d][1].wait_recv()
     acc[...] += product(-1) + product(1)
@@ -124,84 +137,89 @@
                             preferred_element_type=jnp.float32)
     projected = jnp.mean(normed * along, axis=-1, keepdims=True)
     grad_values = ((along - normed * projected) * recip * inv_root).astype(jnp.bfloat16)
-    g_out = []
-    for q in range(SLABS):
-        gsend[q] = grad_values[:, q * cols:(q + 1) * cols]
-        copy = remote(gsend.at[q], grecv.at[q], g_ss.at[q], g_rs.at[q], pair)
-        copy.start()
-        g_out.append(copy)
+    gsend[0] = grad_values[:, :cols]
+    g_out = remote(gsend.at[0], grecv, g_ss.at[0], g_rs.at[0], pair)
+    g_out.start()
+    gsend[1] = grad_values[:, cols:]
+    gx_out = {}
+    for j, peer in turns.items():
+        gx_out[j] = remote(gsend.at[1], grad_x.at[j], gx_ss.at[j], gx_rs.at[j], peer)
+        gx_out[j].start()
     loss = jnp.log(total) + top - chosen
     loss_ref[...] = jnp.transpose(jnp.broadcast_to(loss, (rows, 128)))[0:1, :]
 
-    for q in range(SLABS):
-        for k, of in enumerate((2, 1, -1, 0)):
-            own[q, k] = tdot(tok[:, pl.ds(block(of), depth)], gsend[q]).astype(jnp.bfloat16)
-
-    def summed(q, k, of):
-        other = tdot(tok_y[:, pl.ds(block(of), depth)], grecv[q]).astype(jnp.bfloat16)
-        return own[q, k].astype(jnp.float32) + other.astype(jnp.float32)
+    for k, of in enumerate((2, 1, -1, 0)):
+        own[k] = tdot(tok[:, pl.ds(block(of), depth)], gsend[0]).astype(jnp.bfloat16)
+
+    def summed(k, of):
+        other = tdot(tok_y[:, pl.ds(block(of), depth)], grecv[...]).astype(jnp.bfloat16)
+        return own[k].astype(jnp.float32) + other.astype(jnp.float32)
+
+    def rounded(j, k):
+        values = gsend[1] if j == 0 else grad_x[j]
+        return tdot(tok_x[j, k], values).astype(jnp.bfloat16).astype(jnp.float32)
 
     def half_at(h):
         return pl.ds(h * half, half)
 
-    def opp_copy(q, d):
-        return remote(opp.at[q, half_at(d), :], opp_in.at[q, d], o_ss.at[q, d], o_rs.at[q, d], xs[d])
-
-    def side_copy(q, d, h):
-        return remote(sides.at[q, d, half_at(h), :], side_in.at[q, d, half_at(h), :],
-                      s_ss.at[q, d, h], s_rs.at[q, d, h], xs[d])
-
-    def send_opposite(q):
-        g_out[q].wait_recv()
-        opp[q] = summed(q, 0, 2).astype(jnp.bfloat16)
-        for d in range(2):
-            opp_copy(q, d).start()
-
-    def send_plain(q):
-        for d in range(2):
-            sides[q, d] = summed(q, 1 + d, 1 - 2 * d).astype(jnp.bfloat16)
-            side_copy(q, d, 1 - d).start()
-
-    def send_added(q):
-        for d in range(2):
-            opp_copy(q, d).wait_recv()
-            sides[q, d, half_at(d), :] = (sides[q, d, half_at(d), :].astype(jnp.float32)
-                                          + opp_in[q, d].astype(jnp.float32)).astype(jnp.bfloat16)
-            side_copy(q, d, d).start()
+    def opp_copy(d):
+        return remote(opp.at[half_at(d), :], opp_in.at[d], o_ss.at[d], o_rs.at[d], xs[d])
+
+    def side_copy(d, h):
+        return remote(sides.at[d, half_at(h), :], side_in.at[d, half_at(h), :],
+                      s_ss.at[d, h], s_rs.at[d, h], xs[d])
+
+    x_in[0].wait()
+    x_in[1].wait()
+    for k in range(2):
+        terms[k] = rounded(0, k)
+    g_out.wait_recv()
+    opp[...] = summed(0, 2).astype(jnp.bfloat16)
+    for d in range(2):
+        opp_copy(d).start()
+    for d in range(2):
+        sides[d] = summed(1 + d, 1 - 2 * d).astype(jnp.bfloat16)
+        side_copy(d, 1 - d).start()
+    for i, j in enumerate(turns):
+        x_out[2 * i].wait_recv()
+        x_out[2 * i + 1].wait_recv()
+        gx_out[j].wait_recv()
+        terms[1] += rounded(j, 1)
+    term_out[...] = terms[1].astype(jnp.bfloat16)
+    r_out = remote(term_out, term_in, r_ss.at[0], r_rs.at[0], pair)
+    r_out.start()
+    for d in range(2):
+        opp_copy(d).wait_recv()
+        sides[d, half_at(d), :] = (sides[d, half_at(d), :].astype(jnp.float32)
+                                   + opp_in[d].astype(jnp.float32)).astype(jnp.bfloat16)
+        side_copy(d, d).start()
+    for j in turns:
+        terms[0] += rounded(j, 0)
+    mine[0] = summed(3, 0)
 
     def mix_copy(q):
         return remote(mix_out.at[q], mix_in.at[q], m_ss.at[q], m_rs.at[q], me, ahead)
 
-    def send_updated(q):
-        for d in range(2):
-            for h in range(2):
-                side_copy(q, d, h).wait_recv()
-        grad = mine[q] + side_in[q, 0].astype(jnp.float32) + side_in[q, 1].astype(jnp.float32)
+    def send_updated(q, grad):
         updated = wv[:, q * cols:(q + 1) * cols] - STEP * grad
         mix_out[q] = updated.astype(jnp.bfloat16)
         mix_copy(q).start()
         mine[q] = updated
 
-    for q in range(SLABS):
-        send_opposite(q)
-        if q:
-            send_added(q - 1)
-        send_plain(q)
-        mine[q] = summed(q, 3, 0)
-    send_added(SLABS - 1)
-    for q in range(SLABS):
-        send_updated(q)
-    for q in range(SLABS):
+    r_out.wait_recv()
+    send_updated(1, terms[0] + term_in[...].astype(jnp.float32))
+    for d in range(2):
+        for h in range(2):
+            side_copy(d, h).wait_recv()
+    send_updated(0, mine[0] + side_in[0].astype(jnp.float32) + side_in[1].astype(jnp.float32))
+    for q in (1, 0):
         mix_copy(q).wait_recv()
         mixed_ref[:, q * cols:(q + 1) * cols] = 0.5 * (mine[q] + mix_in[q].astype(jnp.float32))
-    for copy in tok_out + w_out[0] + w_out[1] + p_out + g_out:
+    sent = tok_out + w_out[0] + w_out[1] + p_out + x_out + [g_out, r_out] + list(gx_out.values())
+    for d in range(2):
+        sent += [opp_copy(d), side_copy(d, 0), side_copy(d, 1)]
+    for copy in sent + [mix_copy(0), mix_copy(1)]:
         copy.wait_send()
-    for q in range(SLABS):
-        for d in range(2):
-            opp_copy(q, d).wait_send()
-            for h in range(2):
-                side_copy(q, d, h).wait_send()
-        mix_copy(q).wait_send()
 
 
 def step_call(level, tokens, weights, head, verdict):
@@ -223,15 +241,18 @@
             pltpu.VMEM((depth, kv), f32), pltpu.VMEM((NX * depth, kv), bf16),
             pltpu.VMEM((rows, kv), f32), pltpu.VMEM((rows, grades), f32),
             pltpu.VMEM((rows, kv), bf16), pltpu.VMEM((rows, kv), bf16),
-            pltpu.VMEM((SLABS, rows, cols), bf16), pltpu.VMEM((SLABS, rows, cols), bf16),
-            pltpu.VMEM((SLABS, NX, depth, cols), bf16), pltpu.VMEM((SLABS, depth, cols), f32),
-            pltpu.VMEM((SLABS, depth, cols), bf16), pltpu.VMEM((SLABS, 2, depth, cols), bf16),
-            pltpu.VMEM((SLABS, 2, depth // 2, cols), bf16), pltpu.VMEM((SLABS, 2, depth, cols), bf16),
+            pltpu.VMEM((SLABS, rows, cols), bf16), pltpu.VMEM((rows, cols), bf16),
+            pltpu.VMEM((NX, depth, cols), bf16), pltpu.VMEM((SLABS, depth, cols), f32),
+            pltpu.VMEM((depth, cols), bf16), pltpu.VMEM((2, depth, cols), bf16),
+            pltpu.VMEM((2, depth // 2, cols), bf16), pltpu.VMEM((2, depth, cols), bf16),
             pltpu.VMEM((SLABS, depth, cols), bf16), pltpu.VMEM((SLABS, depth, cols), bf16),
-            sem((2,)), sem((CHUNKS,)), sem((CHUNKS,)), sem((2, 3)), sem((2, 3)),
-            sem((CHUNKS,)), sem((CHUNKS,)), sem((SLABS,)), sem((SLABS,)),
-            sem((SLABS, 2)), sem((SLABS, 2)), sem((SLABS, 2, 2)), sem((SLABS, 2, 2)),
-            sem((SLABS,)), sem((SLABS,)),
+            pltpu.VMEM((NX, 2, rows, depth), bf16), pltpu.VMEM((NX, rows, cols), bf16),
+            pltpu.VMEM((2, depth, cols), f32), pltpu.VMEM((depth, cols), bf16),
+            pltpu.VMEM((depth, cols), bf16),
+            sem((4,)), sem((CHUNKS,)), sem((CHUNKS,)), sem((2, 3)), sem((2, 3)),
+            sem((CHUNKS,)), sem((CHUNKS,)), sem((1,)), sem((1,)),
+            sem((2,)), sem((2,)), sem((2, 2)), sem((2, 2)), sem((SLABS,)), sem((SLABS,)),
+            sem((NX, 2)), sem((NX, 2)), sem((NX,)), sem((NX,)), sem((1,)), sem((1,)),
         ],
         compiler_params=pltpu.CompilerParams(collective_id=level, has_side_effects=True,
                                              vmem_limit_bytes=VMEM_BYTES),

time: 78.9 us -> 95.3 us (1.21)
  the two profiles are of different devices: /device:TPU:16 before, /device:TPU:8 now
where the time goes in v3:
time: 95.3 us; the launch traced here: 95.1 us
  Pallas kernels  91.7 us (96%)
  local copies, waits for them, and re-layouts  1.54 us (2%)
  between operations  1.3 us (1%)
    pallas_call x1, Pallas kernels, step_call(): pl.pallas_call(functools.partial(kernel, wide ** (-0.5), 1 << level), out...  91.7 us

profile of v3, /device:TPU:8, one launch (start us, length us, event | category | flops | bytes accessed | tf_op | source)
XLA Modules:
  0.0 95.1 jit_solution(15057704518398249347)
XLA Ops:
  1.3 92.3 %conditional.1 = ((f32[512,512]{1,0:T(8,128)S(1)}, f32[1,256]{1,0:T(1,128)S(1)})) conditional(s32[]{:T(128)} %clamp.3, (bf16[256,4096]{1,0:T(8,128)(2,1)}, f32[512,512]{1,0:T(8,128)}, bf16[512,128]{1,0:T(8,128)(2,1)}, s32[1,256]{1,0:T(1,128)}) %tuple.71, (bf16[256,4096]{1,0:T(8,128)(2,1)}, f32[512,512]{1,0:T(8,128)}, ...), branch_computations={%region_0.1_spmd, %region_1.2_spmd, %region_2.3_spmd, %region_3.4_... | conditional | bytes 8 | solution.py:266
  1.5 91.7 %step.9 = (f32[512,512]{1,0:T(8,128)S(1)}, f32[1,256]{1,0:T(1,128)S(1)}) custom-call(bf16[256,4096]{1,0:T(8,128)(2,1)} %get-tuple-element.80.tok_hbm, f32[512,512]{1,0:T(8,128)} %get-tuple-element.81.w_hbm, bf16[512,128]{1,0:T(8,128)(2,1)} %get-tuple-element.82.head_ref, s32[1,256]{1,0:T(1,128)} %get-tuple-element.83.verdict_ref), custom_call_target="tpu_custom_call" | custom-call | tf_op jit(solution)/shard_map/cond/branch_3_fun/step/pallas_call | solution.py:234
  93.6 1.0 %copy.22 = f32[1,512,512]{2,1,0:T(8,128)} copy(f32[1,512,512]{2,1,0:T(8,128)S(1)} %bitcast.11) | data formatting | bytes 2097152
  94.6 0.6 copy.23
